TPU v7x, 256 devices: a whole 4x4x8 slice. The times are simulated.
256 devices in a mesh: slide: 16 (over y, x), row: 4 (over z_hi, core), col: 4 (over z_lo).
Axes of the slice: x: 4, y: 4, z: 8 (z_hi: 2, z_lo: 4; z = z_hi * 4 + z_lo), core: 2. Of those that a mesh axis runs over, the one named last changes fastest.
Arguments:
- features: bfloat16 [16, 256, 512, 256], P('slide', 'row', 'col'), may hold values from -6 to 6
- out_grad: bfloat16 [16, 256, 512, 256], P('slide', 'row', 'col'), may hold values from -6 to 6
- depth_weight: bfloat16 [9, 256], replicated, may hold values from -2 to 2
- point_weight: bfloat16 [256, 256], P(('slide', 'row', 'col')), may hold values from -0.375 to 0.375
Outputs:
- feature_grad: bfloat16 [16, 256, 512, 256], P('slide', 'row', 'col')
- point_grad: float32 [256, 256], P(('slide', 'row', 'col'))
- depth_grad: float32 [9, 256], replicated
All inputs are finite; a program needn't handle non-finite values.
Results may differ from a plain program's by a relative error of at most 0.007.
Values may be sent and summed in bfloat16 or wider, within the bound.
No kernel may reach another device: no remote copies, remote signals or barrier semaphores. Data moves between devices by JAX's collectives and lax.ppermute only.
A program may use at most 128 MiB of HBM per device.

v0:
```python
import math
import jax
import jax.numpy as jnp
from jax import lax
from jax.sharding import PartitionSpec as P


def padded(block, sides, width):
    for axis, dim in sides:
        count = lax.axis_size(axis)
        forward = [(i, i + 1) for i in range(count - 1)]
        backward = [(target, source) for source, target in forward]
        low = lax.ppermute(
            lax.slice_in_dim(block, block.shape[dim] - width, None, axis=dim), axis, forward
        )
        high = lax.ppermute(lax.slice_in_dim(block, 0, width, axis=dim), axis, backward)
        block = jnp.concatenate([low, block, high], axis=dim)
    return block


def back_project(grad_flat, point_weight):
    return lax.dot_general(
        grad_flat,
        lax.all_gather(point_weight, ("slide", "row", "col"), axis=0, tiled=True),
        (((1,), (1,)), ((), ())),
        preferred_element_type=jnp.float32,
    ).astype(jnp.bfloat16)


def on_device(features, out_grad, depth_weight, point_weight):
    rows = features.shape[1]
    cols = features.shape[2]
    chans = features.shape[3]
    total = lax.axis_size("slide") * lax.axis_size("row") * lax.axis_size("col") * rows * cols
    scale = 1.0 / math.sqrt(total)
    grad_flat = out_grad[0].reshape(rows * cols, chans)
    feat_pad = padded(features, (("row", 1), ("col", 2)), 2)[0]
    mid_grad = back_project(grad_flat, point_weight).reshape(rows, cols, chans)
    grad_pad = padded(mid_grad[None], (("row", 1), ("col", 2)), 2)[0]
    taps = depth_weight.astype(jnp.float32)
    mid = jnp.zeros((rows, cols, chans), jnp.float32)
    back = jnp.zeros((rows, cols, chans), jnp.float32)
    mid_f = mid_grad.astype(jnp.float32)
    tap_terms = []
    for a in range(3):
        for b in range(3):
            window = feat_pad[2 * a : 2 * a + rows, 2 * b : 2 * b + cols].astype(jnp.float32)
            mid = mid + taps[a * 3 + b] * window
            back = back + taps[a * 3 + b] * grad_pad[
                4 - 2 * a : 4 - 2 * a + rows, 4 - 2 * b : 4 - 2 * b + cols
            ].astype(jnp.float32)
            tap_terms.append(jnp.sum(window * mid_f, axis=(0, 1)))
    mid_flat = mid.astype(jnp.bfloat16).reshape(rows * cols, chans)
    owned = lax.psum_scatter(
        lax.dot_general(
            mid_flat, grad_flat, (((0,), (0,)), ((), ())), preferred_element_type=jnp.float32
        ),
        ("slide", "row", "col"),
        scatter_dimension=0,
        tiled=True,
    )
    depth_grad = lax.psum(jnp.stack(tap_terms), ("slide", "row", "col")) * scale
    feature_grad = back.astype(jnp.bfloat16)[None]
    return (feature_grad, owned * scale, depth_grad)


def solution(mesh):
    placed = (
        P("slide", "row", "col", None),
        P("slide", "row", "col", None),
        P(),
        P(("slide", "row", "col"), None),
    )
    return jax.shard_map(
        on_device,
        mesh=mesh,
        in_specs=placed,
        out_specs=(P("slide", "row", "col", None), P(("slide", "row", "col"), None), P()),
        check_vma=False,
    )
```

profile of v0, /device:TPU:2, one launch (start us, length us, event | category | flops | bytes accessed | tf_op | source)
XLA Modules:
  0.0 971.7 jit_solution(7291026716896225350)
XLA Ops:
  7.2 0.0 all-reduce.3.cloned.1.call-start
  7.2 1.0 fusion.22
  8.2 0.0 copy-start.3
  8.2 1.7 collective-permute-start.4
  10.0 1.3 collective-permute-start.5
  11.3 2.5 constant_dynamic-update-slice_fusion.1
  13.8 6.4 collective-permute-done.5
  20.2 2.1 copy-done.1
  22.3 0.1 fusion.21
  22.4 2.9 collective-permute-start.6
  25.4 1.3 collective-permute-start.7
  26.7 585.9 %all-gather = bf16[256,1,256]{2,1,0:T(2,128)(2,1)S(1)} all-gather(bf16[1,1,256]{2,1,0:T(2,128)(2,1)S(1)} %bitcast.71), channel_id=1, replica_groups=mesh['slide'=16,'row'=4,'col'=4] {'slide','row','col'}, dimensions={0}, use_global_device_ids=true | all-gather | bytes 131584 | tf_op jit(solution)/shard_map/all_gather | solution.py:24
  612.6 0.0 collective-permute-done.6
  612.6 7.2 maximum_bitcast_fusion.1
  619.8 22.3 %fusion.17 = (f32[256]{0:T(256)S(1)}, f32[256]{0:T(256)S(1)}, f32[256]{0:T(256)S(1)}, f32[256]{0:T(256)S(1)}, f32[256]{0:T(256)S(1)}, /*index=5*/f32[256]{0:T(25...) fusion(bf16[68,132,256]{2,1,0:T(8,128)(2,1)} %maximum_bitcast_fusion.1, ...), kind=kOutput, calls=%fused_computation.36 | convolution fusion | flops 1134556928 | bytes 46277632 | tf_op jit(solution)/shard_map/dot_general | solution.py:22
  642.1 0.0 copy-start
  642.1 22.8 %fusion.8 = bf16[64,128,256]{2,1,0:T(8,128)(2,1)S(1)} fusion(f32[256]{0:T(256)S(1)} %bitcast.69, f32[256]{0:T(256)S(1)} %bitcast.67, f32[256]{0:T(256)S(1)} %bitcast.65, f32[256]{0:T(256)S(1)} %bitcast.63, f32[256]{0:T(256)S(1)} %bitcast.61, f32[256]{0:T(256)S(1)} %bitcast.59, f32[256]{0:T(256)S(1)} %bitcast.57, f32[256]{0:T(256)S(1)} %bitcast.55, ...), kind=kLoop, calls=%fused_computation.27 | loop fusion | flops 56623104 | bytes 41952256 | tf_op jit(solution)/shard_map/convert_element_type | solution.py:53
  665.0 2.0 fusion.25
  666.9 0.0 all-reduce.3.cloned.1.call-update
  667.0 111.4 %psum.7 = f32[9,256]{1,0:T(8,128)S(1)} all-reduce(f32[9,256]{1,0:T(8,128)S(1)} %stack.39), channel_id=1, replica_groups=mesh['slide'=16,'row'=4,'col'=4] {'slide','row','col'}, use_global_device_ids=true, to_apply=%region_10.0 | all-reduce | flops 2304 | bytes 18432 | tf_op jit(solution)/shard_map/psum | solution.py:62
  778.4 1.0 fusion.23
  779.4 1.7 collective-permute-start
  781.2 1.3 collective-permute-start.1
  782.5 0.6 broadcast_multiply_fusion
  783.1 2.5 collective-permute-done.1
  785.6 1.1 pad_maximum_fusion.2
  786.7 4.0 collective-permute-start.2
  790.7 1.3 collective-permute-start.3
  792.0 156.4 %all-reduce.3.cloned.1.call-done = f32[256,256]{1,0:T(8,128)} async-done(((f32[256,256]{1,0:T(8,128)}), f32[256,256]{1,0:T(8,128)}) %all-reduce.3.cloned.1.call-update) | async-done | bytes 262160
  948.4 1.3 dynamic-slice_multiply_fusion
  949.7 4.2 maximum_bitcast_fusion
  953.9 10.9 %fusion.18 = bf16[1,64,128,256]{3,2,1,0:T(8,128)(2,1)} fusion(bf16[68,132,256]{2,1,0:T(8,128)(2,1)S(1)} %maximum_bitcast_fusion, f32[256]{0:T(256)S(1)} %bitcast.70, f32[256]{0:T(256)S(1)} %bitcast.68, f32[256]{0:T(256)S(1)} %bitcast.66, f32[256]{0:T(256)S(1)} %bitcast.64, f32[256]{0:T(256)S(1)} %bitcast.62, f32[256]{0:T(256)S(1)} %bitcast.60, ...), kind=kLoop, calls=%fused_computation.40 | loop fusion | flops 56623104 | bytes 41952256 | tf_op jit(solution)/shard_map/broadcast_in_dim | solution.py:63
  (14 shorter events, 0.1 us)
Async XLA Ops:
  7.2 19.5 %copy-start.2 = (bf16[9,256]{1,0:T(8,128)(2,1)S(1)}, bf16[9,256]{1,0:T(8,128)(2,1)}, u32[]{:S(2)}) copy-start(bf16[9,256]{1,0:T(8,128)(2,1)} %param.6) | copy-start | bytes 13828
  7.2 941.2 %all-reduce.3.cloned.1.call-start = ((), (), s32[]{:S(2)}) async-start(), calls=%async_computation | async-start | bytes 524288
  8.2 18.5 %copy-start.3 = (bf16[1,256]{1,0:T(2,128)(2,1)S(1)}, bf16[1,256]{1,0:T(2,128)(2,1)}, u32[]{:S(2)}) copy-start(bf16[1,256]{1,0:T(2,128)(2,1)} %param.7) | copy-start | bytes 1540
  8.2 3.1 collective-permute-start.4
  10.0 10.2 %collective-permute-start.5 = (bf16[1,2,128,256]{3,2,1,0:T(8,128)(2,1)S(1)}, bf16[1,2,128,256]{3,2,1,0:T(8,128)(2,1)S(1)}, u32[]{:S(2)}, u32[]{:S(2)}) collective-permute-start(bf16[1,2,128,256]{3,2,1,0:T(8,128)(2,1)S(1)} %get-tuple-element.16), channel_id=1, source_target_pairs={{4,0},{8,4},{12,8},{5,1},{9,5},{13,9},{6,2},{10,6},{14,10},{7,3},{... | collective-permute-start | bytes 393224 | tf_op jit(solution)/shard_map/ppermute | solution.py:16
  20.2 2.1 copy-start.1
  22.4 590.2 %collective-permute-start.6 = (bf16[1,68,2,256]{3,2,1,0:T(2,128)(2,1)S(1)}, bf16[1,68,2,256]{3,2,1,0:T(2,128)(2,1)S(1)}, u32[]{:S(2)}, u32[]{:S(2)}) collective-permute-start(bf16[1,68,2,256]{3,2,1,0:T(2,128)(2,1)S(1)} %get-tuple-element.12), channel_id=1, source_target_pairs={{0,1},{1,2},{2,3},{4,5},{5,6},{6,7},{8,9},{9,10},{10,11},{12,13},{... | collective-permute-start | bytes 208904 | tf_op jit(solution)/shard_map/ppermute | solution.py:13
  25.4 587.2 %collective-permute-start.7 = (bf16[1,68,2,256]{3,2,1,0:T(2,128)(2,1)S(1)}, bf16[1,68,2,256]{3,2,1,0:T(2,128)(2,1)S(1)}, u32[]{:S(2)}, u32[]{:S(2)}) collective-permute-start(bf16[1,68,2,256]{3,2,1,0:T(2,128)(2,1)S(1)} %get-tuple-element.13), channel_id=1, source_target_pairs={{1,0},{2,1},{3,2},{5,4},{6,5},{7,6},{9,8},{10,9},{11,10},{13,12},{... | collective-permute-start | bytes 208904 | tf_op jit(solution)/shard_map/ppermute | solution.py:16
  642.1 22.8 %copy-start = (bf16[1,64,128,256]{3,2,1,0:T(8,128)(2,1)S(1)}, bf16[1,64,128,256]{3,2,1,0:T(8,128)(2,1)}, u32[]{:S(2)}) copy-start(bf16[1,64,128,256]{3,2,1,0:T(8,128)(2,1)} %param.5) | copy-start | bytes 12582916
  779.4 3.7 collective-permute-start
  781.2 4.4 collective-permute-start.1
  786.7 162.9 %collective-permute-start.2 = (bf16[1,68,2,256]{3,2,1,0:T(2,128)(2,1)S(1)}, bf16[1,68,2,256]{3,2,1,0:T(2,128)(2,1)S(1)}, u32[]{:S(2)}, u32[]{:S(2)}) collective-permute-start(bf16[1,68,2,256]{3,2,1,0:T(2,128)(2,1)S(1)} %get-tuple-element.14), channel_id=1, source_target_pairs={{0,1},{1,2},{2,3},{4,5},{5,6},{6,7},{8,9},{9,10},{10,11},{12,13},{... | collective-permute-start | bytes 208904 | tf_op jit(solution)/shard_map/ppermute | solution.py:13
  790.7 158.9 %collective-permute-start.3 = (bf16[1,68,2,256]{3,2,1,0:T(2,128)(2,1)S(1)}, bf16[1,68,2,256]{3,2,1,0:T(2,128)(2,1)S(1)}, u32[]{:S(2)}, u32[]{:S(2)}) collective-permute-start(bf16[1,68,2,256]{3,2,1,0:T(2,128)(2,1)S(1)} %get-tuple-element.15), channel_id=1, source_target_pairs={{1,0},{2,1},{3,2},{5,4},{6,5},{7,6},{9,8},{10,9},{11,10},{13,12},{... | collective-permute-start | bytes 208904 | tf_op jit(solution)/shard_map/ppermute | solution.py:16
Sparse Core Ops, SparseCore 0:
  667.1 281.2 all-reduce.2
where the time goes:
time: 972 us
  blocking collectives  697 us (72%)
  waiting for transfers between devices  165 us (17%)
  other arithmetic  48.2 us (5%)
  matrix products  24.3 us (2%)
  starting transfers between devices  15.6 us (2%)
  between operations  14.2 us (1%)
    all_gather x1, blocking collectives, back_project(): lax.all_gather(point_weight, ('slide', 'row', 'col'), axis=0, tiled=True)  586 us
    unnamed x2, waiting for transfers between devices  156 us
    psum x1, blocking collectives, on_device(): depth_grad = lax.psum(jnp.stack(tap_terms), ('slide', 'row', 'col')) * scale  111 us
    convert_element_type x1, other arithmetic, on_device(): mid_flat = mid.astype(jnp.bfloat16).reshape(rows * cols, chans)  22.8 us
    dot_general x1, matrix products, back_project(): lax.dot_general(grad_flat, lax.all_gather(point_weight, ('slide', 'row',...  22.3 us
  transfers between devices with their start and end apart: 9, of which 3 were waited for; matrix products, arithmetic and copies ran while one was open for 1% of the time, Pallas kernels for 0%

commit v1 on v0

--- a/solution.py
+++ b/solution.py
@@ -19,9 +19,19 @@
 
 
 def back_project(grad_flat, point_weight):
+
+    def form_trees(u):
+        p_next = lax.all_to_all(
+            jnp.stack([u for _ in range(lax.psum(1, ("slide", "row", "col")))]),
+            ("slide", "row", "col"),
+            0,
+            0,
+        )
+        return jnp.concatenate(p_next, axis=0)
+
     return lax.dot_general(
         grad_flat,
-        lax.all_gather(point_weight, ("slide", "row", "col"), axis=0, tiled=True),
+        form_trees(point_weight),
         (((1,), (1,)), ((), ())),
         preferred_element_type=jnp.float32,
     ).astype(jnp.bfloat16)

time: 972 us -> 340 us (0.35)
  blocking collectives: 697 us -> 82.1 us
  waiting for transfers between devices: 165 us -> 145 us
  starting transfers between devices: 15.6 us -> 31.8 us
  other arithmetic: 48.2 us -> 34.5 us
    all_gather x1 -> x0, blocking collectives: 586 us -> none  [back_project(): lax.all_gather(point_weight, ('slide', 'row', 'col'), axis=0, tiled=True)]
    psum x1, blocking collectives: 111 us -> 82.1 us  [on_device(): depth_grad = lax.psum(jnp.stack(tap_terms), ('slide', 'row', 'col')) * scale]
    unnamed x2, waiting for transfers between devices: 156 us -> 137 us
    all_to_all x0 -> x1, starting transfers between devices: none -> 16.5 us  [form_trees(): lax.all_to_all(jnp.stack([u for _ in range(lax.psum(1, ('slide', 'row', '...]
    convert_element_type x1, other arithmetic: 22.8 us -> 9.92 us  [on_device(): mid_flat = mid.astype(jnp.bfloat16).reshape(rows * cols, chans)]
  transfers between devices with their start and end apart: 9 -> 10, of which waited for: 3 -> 4; matrix products, arithmetic and copies ran while one was open for 1% -> 14% of each run, Pallas kernels for 0% -> 0%
where the time goes in v1:
time: 340 us
  waiting for transfers between devices  145 us (43%)
  blocking collectives  82.1 us (24%)
  other arithmetic  34.5 us (10%)
  starting transfers between devices  31.8 us (9%)
  matrix products  24.2 us (7%)
  between operations  14.3 us (4%)
  local copies, waits for them, and re-layouts  8.06 us (2%)
    unnamed x2, waiting for transfers between devices  137 us
    psum x1, blocking collectives, on_device(): depth_grad = lax.psum(jnp.stack(tap_terms), ('slide', 'row', 'col')) * scale  82.1 us
    dot_general x1, matrix products, back_project(): lax.dot_general(grad_flat, form_trees(point_weight), (((1,), (1,)), ((),...  22.2 us
    all_to_all x1, starting transfers between devices, form_trees(): lax.all_to_all(jnp.stack([u for _ in range(lax.psum(1, ('slide', 'row', '...  16.5 us
    broadcast_in_dim x1, other arithmetic, on_device(): feature_grad = back.astype(jnp.bfloat16)[None]  10.9 us
    convert_element_type x1, other arithmetic, on_device(): mid_flat = mid.astype(jnp.bfloat16).reshape(rows * cols, chans)  9.92 us
    ppermute x4, starting transfers between devices, padded(): lax.ppermute(lax.slice_in_dim(block, block.shape[dim] - width, None, axis...  9.86 us
    ppermute x4, waiting for transfers between devices, padded(): lax.ppermute(lax.slice_in_dim(block, 0, width, axis=dim), axis, backward)  7.1 us
  transfers between devices with their start and end apart: 10, of which 4 were waited for; matrix products, arithmetic and copies ran while one was open for 14% of the time, Pallas kernels for 0%

profile of v1, /device:TPU:2, one launch (start us, length us, event | category | flops | bytes accessed | tf_op | source)
XLA Modules:
  0.0 339.6 jit_solution(11864813117959371998)
XLA Ops:
  7.2 1.0 fusion.22
  8.2 1.7 collective-permute-start.4
  9.9 0.7 reduce
  10.6 0.1 stack.22
  10.8 0.5 broadcast.4
  11.3 1.4 reduce.1
  12.7 0.7 reshape.31
  13.4 16.5 %all-to-all-start = ((bf16[256,2,128]{2,1,0:T(2,128)(2,1)}), bf16[256,2,128]{2,1,0:T(2,128)(2,1)S(1)}, u32[]{:S(2)}, u32[]{:S(2)}) async-start(bf16[256,2,128]{2,1,0:T(2,128)(2,1)} %reshape.31), calls=%async_computation | async-start | bytes 262144 | tf_op jit(solution)/shard_map/all_to_all | solution.py:24
  29.9 1.3 collective-permute-start.5
  31.3 2.5 constant_dynamic-update-slice_fusion.1
  33.8 2.0 copy-done.2
  35.9 3.5 %collective-permute-start.6 = (bf16[1,68,2,256]{3,2,1,0:T(2,128)(2,1)S(1)}, bf16[1,68,2,256]{3,2,1,0:T(2,128)(2,1)S(1)}, u32[]{:S(2)}, u32[]{:S(2)}) collective-permute-start(bf16[1,68,2,256]{3,2,1,0:T(2,128)(2,1)S(1)} %get-tuple-element.12), channel_id=1, source_target_pairs={{0,1},{1,2},{2,3},{4,5},{5,6},{6,7},{8,9},{9,10},{10,11},{12,13},{... | collective-permute-start | bytes 208904 | tf_op jit(solution)/shard_map/ppermute | solution.py:13
  39.4 1.5 collective-permute-start.7
  40.9 1.1 collective-permute-done.6
  42.0 3.6 %collective-permute-done.7 = bf16[1,68,2,256]{3,2,1,0:T(2,128)(2,1)S(1)} collective-permute-done((bf16[1,68,2,256]{3,2,1,0:T(2,128)(2,1)S(1)}, bf16[1,68,2,256]{3,2,1,0:T(2,128)(2,1)S(1)}, u32[]{:S(2)}, u32[]{:S(2)}) %collective-permute-start.7) | collective-permute-done | bytes 69664 | tf_op jit(solution)/shard_map/ppermute | solution.py:16
  45.6 4.3 %maximum_bitcast_fusion.1 = bf16[68,132,256]{2,1,0:T(8,128)(2,1)S(1)} fusion(bf16[1,68,2,256]{3,2,1,0:T(2,128)(2,1)S(1)} %collective-permute-done.7, bf16[1,68,128,256]{3,2,1,0:T(8,128)(2,1)} %copy-done.2, bf16[1,68,2,256]{3,2,1,0:T(2,128)(2,1)S(1)} %collective-permute-done.6), kind=kLoop, calls=%fused_computation.39 | loop fusion | flops 13787136 | bytes 9191424 | tf_op jit(solution)/shard_map/squeeze | solution.py:47
  49.9 9.9 %fusion.8 = bf16[64,128,256]{2,1,0:T(8,128)(2,1)S(1)} fusion(f32[256]{0:T(256)S(1)} %bitcast.68, f32[256]{0:T(256)S(1)} %bitcast.66, f32[256]{0:T(256)S(1)} %bitcast.64, f32[256]{0:T(256)S(1)} %bitcast.62, f32[256]{0:T(256)S(1)} %bitcast.60, f32[256]{0:T(256)S(1)} %bitcast.58, f32[256]{0:T(256)S(1)} %bitcast.56, f32[256]{0:T(256)S(1)} %bitcast.54, ...), kind=kLoop, calls=%fused_computation.27 | loop fusion | flops 56623104 | bytes 41952256 | tf_op jit(solution)/shard_map/convert_element_type | solution.py:63
  59.9 2.0 fusion.25
  62.0 22.2 %fusion.17 = (f32[256]{0:T(256)S(1)}, f32[256]{0:T(256)S(1)}, f32[256]{0:T(256)S(1)}, f32[256]{0:T(256)S(1)}, f32[256]{0:T(256)S(1)}, /*index=5*/f32[256]{0:T(25...) fusion(bf16[68,132,256]{2,1,0:T(8,128)(2,1)} %copy-done, ...), kind=kOutput, calls=%fused_computation.36 | convolution fusion | flops 1134556928 | bytes 46277632 | tf_op jit(solution)/shard_map/dot_general | solution.py:32
  84.2 82.1 %psum.7 = f32[9,256]{1,0:T(8,128)S(1)} all-reduce(f32[9,256]{1,0:T(8,128)S(1)} %stack.32), channel_id=1, replica_groups=mesh['slide'=16,'row'=4,'col'=4] {'slide','row','col'}, use_global_device_ids=true, to_apply=%region_10.0 | all-reduce | flops 2304 | bytes 18432 | tf_op jit(solution)/shard_map/psum | solution.py:72
  166.3 1.0 fusion.23
  167.3 1.5 collective-permute-start
  168.8 1.3 collective-permute-start.1
  170.1 0.6 broadcast_multiply_fusion
  170.7 3.5 %collective-permute-done.1 = bf16[1,2,128,256]{3,2,1,0:T(8,128)(2,1)S(1)} collective-permute-done((bf16[1,2,128,256]{3,2,1,0:T(8,128)(2,1)S(1)}, bf16[1,2,128,256]{3,2,1,0:T(8,128)(2,1)S(1)}, u32[]{:S(2)}, u32[]{:S(2)}) %collective-permute-start.1) | collective-permute-done | bytes 131104 | tf_op jit(solution)/shard_map/ppermute | solution.py:16
  174.2 1.1 pad_maximum_fusion.2
  175.3 3.1 collective-permute-start.2
  178.5 1.3 collective-permute-start.3
  179.8 136.6 %all-reduce.3.cloned.1.call-done = f32[256,256]{1,0:T(8,128)} async-done(((f32[256,256]{1,0:T(8,128)}), f32[256,256]{1,0:T(8,128)}) %all-reduce.3.cloned.1.call-update) | async-done | bytes 262160
  316.3 1.3 dynamic-slice_multiply_fusion
  317.6 4.2 %maximum_bitcast_fusion = bf16[68,132,256]{2,1,0:T(8,128)(2,1)S(1)} fusion(bf16[1,68,2,256]{3,2,1,0:T(2,128)(2,1)S(1)} %collective-permute-done.3, bf16[1,2,128,256]{3,2,1,0:T(8,128)(2,1)S(1)} %collective-permute-done.1, bf16[1,64,128,256]{3,2,1,0:T(8,128)(2,1)} %bitcast.49, bf16[1,2,128,256]{3,2,1,0:T(8,128)(2,1)S(1)} %collective-permute-done, ...), kind=kLoop, calls=%fused_computation.38 | loop fusion | flops 22978560 | bytes 9191424 | tf_op jit(solution)/shard_map/squeeze | solution.py:49
  321.8 10.9 %fusion.18 = bf16[1,64,128,256]{3,2,1,0:T(8,128)(2,1)} fusion(bf16[68,132,256]{2,1,0:T(8,128)(2,1)S(1)} %maximum_bitcast_fusion, f32[256]{0:T(256)S(1)} %bitcast.69, f32[256]{0:T(256)S(1)} %bitcast.67, f32[256]{0:T(256)S(1)} %bitcast.65, f32[256]{0:T(256)S(1)} %bitcast.63, f32[256]{0:T(256)S(1)} %bitcast.61, f32[256]{0:T(256)S(1)} %bitcast.59, ...), kind=kLoop, calls=%fused_computation.40 | loop fusion | flops 56623104 | bytes 41952256 | tf_op jit(solution)/shard_map/broadcast_in_dim | solution.py:73
  (21 shorter events, 0.3 us)
Async XLA Ops:
  8.2 23.1 %collective-permute-start.4 = (bf16[1,2,128,256]{3,2,1,0:T(8,128)(2,1)S(1)}, bf16[1,2,128,256]{3,2,1,0:T(8,128)(2,1)S(1)}, u32[]{:S(2)}, u32[]{:S(2)}) collective-permute-start(bf16[1,2,128,256]{3,2,1,0:T(8,128)(2,1)S(1)} %get-tuple-element.17), channel_id=1, source_target_pairs={{0,4},{4,8},{8,12},{1,5},{5,9},{9,13},{2,6},{6,10},{10,14},{3,7},{... | collective-permute-start | bytes 393224 | tf_op jit(solution)/shard_map/ppermute | solution.py:13
  13.4 27.5 %copy-start.3 = (bf16[9,256]{1,0:T(8,128)(2,1)S(1)}, bf16[9,256]{1,0:T(8,128)(2,1)}, u32[]{:S(2)}) copy-start(bf16[9,256]{1,0:T(8,128)(2,1)} %param.6) | copy-start | bytes 13828
  13.4 48.6 %all-to-all-start = ((bf16[256,2,128]{2,1,0:T(2,128)(2,1)}), bf16[256,2,128]{2,1,0:T(2,128)(2,1)S(1)}, u32[]{:S(2)}, u32[]{:S(2)}) async-start(bf16[256,2,128]{2,1,0:T(2,128)(2,1)} %reshape.31), calls=%async_computation | async-start | bytes 262144 | tf_op jit(solution)/shard_map/all_to_all | solution.py:24
  29.9 286.4 %all-reduce.3.cloned.1.call-start = ((), (), s32[]{:S(2)}) async-start(), calls=%async_computation.1 | async-start | bytes 524288
  29.9 3.8 %collective-permute-start.5 = (bf16[1,2,128,256]{3,2,1,0:T(8,128)(2,1)S(1)}, bf16[1,2,128,256]{3,2,1,0:T(8,128)(2,1)S(1)}, u32[]{:S(2)}, u32[]{:S(2)}) collective-permute-start(bf16[1,2,128,256]{3,2,1,0:T(8,128)(2,1)S(1)} %get-tuple-element.16), channel_id=1, source_target_pairs={{4,0},{8,4},{12,8},{5,1},{9,5},{13,9},{6,2},{10,6},{14,10},{7,3},{... | collective-permute-start | bytes 393224 | tf_op jit(solution)/shard_map/ppermute | solution.py:16
  33.8 2.0 copy-start.2
  35.9 6.1 %collective-permute-start.6 = (bf16[1,68,2,256]{3,2,1,0:T(2,128)(2,1)S(1)}, bf16[1,68,2,256]{3,2,1,0:T(2,128)(2,1)S(1)}, u32[]{:S(2)}, u32[]{:S(2)}) collective-permute-start(bf16[1,68,2,256]{3,2,1,0:T(2,128)(2,1)S(1)} %get-tuple-element.12), channel_id=1, source_target_pairs={{0,1},{1,2},{2,3},{4,5},{5,6},{6,7},{8,9},{9,10},{10,11},{12,13},{... | collective-permute-start | bytes 208904 | tf_op jit(solution)/shard_map/ppermute | solution.py:13
  39.4 6.2 %collective-permute-start.7 = (bf16[1,68,2,256]{3,2,1,0:T(2,128)(2,1)S(1)}, bf16[1,68,2,256]{3,2,1,0:T(2,128)(2,1)S(1)}, u32[]{:S(2)}, u32[]{:S(2)}) collective-permute-start(bf16[1,68,2,256]{3,2,1,0:T(2,128)(2,1)S(1)} %get-tuple-element.13), channel_id=1, source_target_pairs={{1,0},{2,1},{3,2},{5,4},{6,5},{7,6},{9,8},{10,9},{11,10},{13,12},{... | collective-permute-start | bytes 208904 | tf_op jit(solution)/shard_map/ppermute | solution.py:16
  49.9 10.0 %copy-start = (bf16[68,132,256]{2,1,0:T(8,128)(2,1)}, bf16[68,132,256]{2,1,0:T(8,128)(2,1)S(1)}, u32[]{:S(2)}) copy-start(bf16[68,132,256]{2,1,0:T(8,128)(2,1)S(1)} %maximum_bitcast_fusion.1) | copy-start | bytes 13787140
  49.9 10.0 %copy-start.1 = (bf16[1,64,128,256]{3,2,1,0:T(8,128)(2,1)S(1)}, bf16[1,64,128,256]{3,2,1,0:T(8,128)(2,1)}, u32[]{:S(2)}) copy-start(bf16[1,64,128,256]{3,2,1,0:T(8,128)(2,1)} %param.5) | copy-start | bytes 12582916
  167.3 3.4 %collective-permute-start = (bf16[1,2,128,256]{3,2,1,0:T(8,128)(2,1)S(1)}, bf16[1,2,128,256]{3,2,1,0:T(8,128)(2,1)S(1)}, u32[]{:S(2)}, u32[]{:S(2)}) collective-permute-start(bf16[1,2,128,256]{3,2,1,0:T(8,128)(2,1)S(1)} %get-tuple-element.18), channel_id=1, source_target_pairs={{0,4},{4,8},{8,12},{1,5},{5,9},{9,13},{2,6},{6,10},{10,14},{3,7},{... | collective-permute-start | bytes 393224 | tf_op jit(solution)/shard_map/ppermute | solution.py:13
  168.8 5.4 %collective-permute-start.1 = (bf16[1,2,128,256]{3,2,1,0:T(8,128)(2,1)S(1)}, bf16[1,2,128,256]{3,2,1,0:T(8,128)(2,1)S(1)}, u32[]{:S(2)}, u32[]{:S(2)}) collective-permute-start(bf16[1,2,128,256]{3,2,1,0:T(8,128)(2,1)S(1)} %get-tuple-element.19), channel_id=1, source_target_pairs={{4,0},{8,4},{12,8},{5,1},{9,5},{13,9},{6,2},{10,6},{14,10},{7,3},{... | collective-permute-start | bytes 393224 | tf_op jit(solution)/shard_map/ppermute | solution.py:16
  175.3 142.2 %collective-permute-start.2 = (bf16[1,68,2,256]{3,2,1,0:T(2,128)(2,1)S(1)}, bf16[1,68,2,256]{3,2,1,0:T(2,128)(2,1)S(1)}, u32[]{:S(2)}, u32[]{:S(2)}) collective-permute-start(bf16[1,68,2,256]{3,2,1,0:T(2,128)(2,1)S(1)} %get-tuple-element.14), channel_id=1, source_target_pairs={{0,1},{1,2},{2,3},{4,5},{5,6},{6,7},{8,9},{9,10},{10,11},{12,13},{... | collective-permute-start | bytes 208904 | tf_op jit(solution)/shard_map/ppermute | solution.py:13
  178.5 139.1 %collective-permute-start.3 = (bf16[1,68,2,256]{3,2,1,0:T(2,128)(2,1)S(1)}, bf16[1,68,2,256]{3,2,1,0:T(2,128)(2,1)S(1)}, u32[]{:S(2)}, u32[]{:S(2)}) collective-permute-start(bf16[1,68,2,256]{3,2,1,0:T(2,128)(2,1)S(1)} %get-tuple-element.15), channel_id=1, source_target_pairs={{1,0},{2,1},{3,2},{5,4},{6,5},{7,6},{9,8},{10,9},{11,10},{13,12},{... | collective-permute-start | bytes 208904 | tf_op jit(solution)/shard_map/ppermute | solution.py:16
Sparse Core Ops, SparseCore 0:
  62.1 254.2 all-reduce.2
